TPU v7x, 32 devices: a whole 2x2x4 slice. The times are simulated.
32 devices in a mesh: expert: 4 (over z), dp: 8 (over y, x, core).
Axes of the slice: x: 2, y: 2, z: 4, core: 2. Of those that a mesh axis runs over, the one named last changes fastest.
Arguments:
- tokens: bfloat16 [3072, 2304], P(('expert', 'dp')), may hold values from -6 to 6
- expert_ids: int32 [3072, 2], P(('expert', 'dp')), may hold values from 0 to 3, all different within a row; in each aligned block of 96 rows (0 to 95, 96 to 191, ...) at most 64 rows name the same one
- gate_weights: float32 [3072, 2], P(('expert', 'dp')), may hold values from 0.2 to 1
- request_lengths: int32 [32, 4], P(('expert', 'dp')), may hold values from 1 to 48, 96 in all within a row
- request_adapter: int32 [32, 4], P(('expert', 'dp')), may hold values from 0 to 63
- expert_weights: bfloat16 [4, 2, 2304, 5760], P('expert', None, None, 'dp'), may hold values from -0.125 to 0.125
- expert_down: bfloat16 [4, 5760, 2304], P('expert', 'dp'), may hold values from -0.078125 to 0.078125
- low_down: bfloat16 [4, 2304, 2048], P('expert', None, 'dp'), may hold values from -0.125 to 0.125
- low_up: bfloat16 [4, 2, 1024, 5760], P('expert', None, None, 'dp'), may hold values from -1.5 to 1.5
Outputs:
- mixed: bfloat16 [3072, 2304], P(('expert', 'dp'))
Inputs may be any that keep to these rules, and one draw needn't show every extreme that they name: `expert_ids`: each row names 2 different experts; within the rows of one device no expert is named by more than 64 rows, a bound that some block reaches. `request_lengths`: each row sums to 96, and its largest entry is exactly 48.
All inputs are finite; a program needn't handle non-finite values.
Results may differ from a plain program's by a relative error of at most 0.017.
Values may be sent and summed in bfloat16 or wider, within the bound.
No kernel may reach another device: no remote copies, remote signals or barrier semaphores. Data moves between devices by JAX's collectives and lax.ppermute only.
A program may use at most 192 MiB of HBM per device.

v0:
```python
import jax
import jax.numpy as jnp
from jax import lax
from jax.sharding import PartitionSpec as P

TOP = 2
RANK = 16


def body(
    tokens,
    expert_ids,
    gate_weights,
    request_lengths,
    request_adapter,
    expert_weights,
    expert_down,
    low_down,
    low_up,
):
    ways_expert = lax.axis_size("expert")
    local_tokens = tokens.shape[0]
    width = tokens.shape[1]
    experts_all = ways_expert * expert_down.shape[0]
    capacity = local_tokens * TOP * 4 // (3 * experts_all)
    slots_all = experts_all * capacity
    held = low_down.shape[2] // (2 * RANK)
    adapters_all = low_up.shape[2] // RANK
    values = tokens.astype(jnp.float32)
    normed = (values * lax.rsqrt(jnp.mean(values * values, axis=1, keepdims=True) + 1e-05)).astype(
        jnp.bfloat16
    )
    ends = jnp.cumsum(request_lengths[0])
    place = jnp.arange(local_tokens, dtype=jnp.int32)
    which = jnp.sum((place[:, None] >= ends[None, :]).astype(jnp.int32), axis=1)
    lookup = (
        which[:, None] == jnp.arange(request_lengths.shape[1], dtype=jnp.int32)[None, :]
    ).astype(jnp.int32)
    adapter = jnp.sum(lookup * request_adapter[0][None, :], axis=1)
    flat = expert_ids.reshape(-1)
    onehot = (flat[:, None] == jnp.arange(experts_all, dtype=jnp.int32)[None, :]).astype(jnp.int32)
    slot = jnp.sum((jnp.cumsum(onehot, axis=0) - onehot) * onehot, axis=1)
    target = flat * capacity + slot
    placement_weights = (jnp.arange(slots_all, dtype=jnp.int32)[:, None] == target[None, :]).astype(
        jnp.bfloat16
    )
    pairs = jnp.repeat(normed, TOP, axis=0)
    outgoing = (
        jnp.dot(placement_weights, pairs, preferred_element_type=jnp.float32)
        .astype(jnp.bfloat16)
        .reshape(experts_all, capacity, width)
    )
    pair_adapter = jnp.repeat(adapter, TOP).astype(jnp.float32)
    outgoing_ids = (
        jnp.dot(placement_weights.astype(jnp.float32), pair_adapter)
        .astype(jnp.bfloat16)
        .reshape(experts_all, capacity)
    )
    arrived, arrived_ids = (
        lax.all_to_all(outgoing, "expert", split_axis=0, concat_axis=0, tiled=True),
        lax.all_to_all(outgoing_ids, "expert", split_axis=0, concat_axis=0, tiled=True),
    )
    rows, labels_wire = (
        lax.all_gather(arrived.reshape(-1, width), "dp", axis=0, tiled=True),
        lax.all_gather(arrived_ids.reshape(-1), "dp", axis=0, tiled=True),
    )
    rows_total = rows.shape[0]
    labels = labels_wire.astype(jnp.int32)
    group = lax.axis_index("dp")
    projected = jnp.dot(rows, low_down[0], preferred_element_type=jnp.float32).reshape(
        rows_total, held, 2 * RANK
    )
    owned = (labels[:, None] == group * held + jnp.arange(held, dtype=jnp.int32)[None, :]).astype(
        jnp.float32
    )
    lowrank_part = jnp.sum(owned[:, :, None] * projected, axis=1)
    lowrank = lax.psum(lowrank_part.astype(jnp.bfloat16), "dp")
    marks = (labels[:, None] == jnp.arange(adapters_all, dtype=jnp.int32)[None, :]).astype(
        jnp.bfloat16
    )
    spread_gate = (marks[:, :, None] * lowrank[:, None, :RANK]).reshape(
        lax.axis_size("dp") * (ways_expert * capacity), adapters_all * RANK
    )
    sharded_up_weight = (marks[:, :, None] * lowrank[:, None, RANK:]).reshape(
        lax.axis_size("dp") * (ways_expert * capacity), adapters_all * RANK
    )
    gate = jnp.dot(rows, expert_weights[0, 0], preferred_element_type=jnp.float32) + jnp.dot(
        spread_gate, low_up[0, 0], preferred_element_type=jnp.float32
    )
    up = jnp.dot(rows, expert_weights[0, 1], preferred_element_type=jnp.float32) + jnp.dot(
        sharded_up_weight, low_up[0, 1], preferred_element_type=jnp.float32
    )
    hidden_activations = (jax.nn.silu(gate) * up).astype(jnp.bfloat16)
    mine = lax.psum_scatter(
        jnp.dot(hidden_activations, expert_down[0], preferred_element_type=jnp.float32).astype(
            jnp.bfloat16
        ),
        "dp",
        scatter_dimension=0,
        tiled=True,
    ).astype(jnp.float32)
    mine = mine.astype(jnp.bfloat16).reshape(ways_expert, capacity, width)
    back = lax.all_to_all(mine, "expert", split_axis=0, concat_axis=0, tiled=True)
    picked = jnp.dot(
        placement_weights.T, back.reshape(slots_all, width), preferred_element_type=jnp.float32
    ).reshape(local_tokens, TOP, width)
    mixed = values + jnp.sum(gate_weights[:, :, None] * picked, axis=1)
    return mixed.astype(jnp.bfloat16)


def solution(mesh):
    return jax.shard_map(
        body,
        mesh=mesh,
        in_specs=(
            P(("expert", "dp"), None),
            P(("expert", "dp"), None),
            P(("expert", "dp"), None),
            P(("expert", "dp"), None),
            P(("expert", "dp"), None),
            P("expert", None, None, "dp"),
            P("expert", "dp", None),
            P("expert", None, "dp"),
            P("expert", None, None, "dp"),
        ),
        out_specs=P(("expert", "dp"), None),
        check_vma=False,
    )
```

profile of v0, /device:TPU:0, one launch (start us, length us, event | category | flops | bytes accessed | tf_op | source)
XLA Modules:
  0.0 319.4 jit_solution(102362111478720045)
XLA Ops:
  7.6 1.2 reduce-window.18
  9.3 1.2 fusion.24
  10.5 1.2 fusion.25
  11.7 1.4 broadcast_in_dim.4
  13.1 3.1 reshape.195
  16.2 1.6 convolution_convert_fusion.1
  17.9 34.8 %all_to_all.20 = bf16[4,64,2304]{2,1,0:T(8,128)(2,1)} all-to-all(bf16[4,64,2304]{2,1,0:T(8,128)(2,1)S(1)} %bitcast.58), channel_id=1, replica_groups=mesh['expert'=4,'dp'=8] {'expert'}, dimensions={0} | all-to-all | bytes 2359296 | tf_op jit(solution)/shard_map/all_to_all | solution.py:60
  54.1 3.2 %all-to-all-start.1 = ((bf16[4,1,64]{2,1,0:T(2,128)(2,1)}), bf16[4,1,64]{2,1,0:T(2,128)(2,1)S(1)}, u32[]{:S(2)}, u32[]{:S(2)}) async-start(bf16[4,1,64]{2,1,0:T(2,128)(2,1)} %all_to_all.16), calls=%async_computation.1 | async-start | bytes 4096 | tf_op jit(solution)/shard_map/all_to_all | solution.py:61
  57.4 2.4 copy.28
  59.9 2.9 all-to-all-done.1
  62.9 8.9 %all-gather = bf16[8,1,256]{2,1,0:T(2,128)(2,1)S(1)} all-gather(bf16[1,1,256]{2,1,0:T(2,128)(2,1)S(1)} %reshape.204), channel_id=1, replica_groups=mesh['expert'=4,'dp'=8] {'dp'}, dimensions={0}, use_global_device_ids=true | all-gather | bytes 4608 | tf_op jit(solution)/shard_map/all_gather | solution.py:65
  72.6 38.1 %all-gather.3.cloned.1.call-done = bf16[2048,2304]{1,0:T(8,128)(2,1)} async-done(((bf16[256,2304]{1,0:T(8,128)(2,1)}), bf16[2048,2304]{1,0:T(8,128)(2,1)}) %all-gather.3.cloned.1.call-update) | async-done | bytes 9437200 | tf_op jit(solution)/shard_map/all_gather | solution.py:64
  110.8 7.3 %fusion.21 = bf16[2048,32]{0,1:T(8,128)(2,1)} fusion(bf16[8,32,2304]{2,1,0:T(8,128)(2,1)} %bitcast.62, bf16[2048,2304]{1,0:T(8,128)(2,1)} %all-gather.3.cloned.1.call-done, f32[2048,8]{0,1:T(8,128)S(1)} %compare_convert_fusion), kind=kOutput, calls=%fused_computation.23 | convolution fusion | flops 2416902144 | bytes 10813440 | tf_op jit(solution)/shard_map/dot_general | solution.py:70
  118.3 12.2 %fusion.3 = f32[2048,720]{0,1:T(8,128)} fusion(bf16[2048,2304]{1,0:T(8,128)(2,1)} %all-gather.3.cloned.1.call-done, bf16[1,2,2304,720]{2,3,1,0:T(8,128)(2,1)} %param.14), kind=kOutput, calls=%fused_computation.7 | convolution fusion | flops 6794772480 | bytes 18653184 | tf_op jit(solution)/shard_map/dot_general | solution.py:90
  130.5 12.2 %fusion.5 = f32[2048,720]{0,1:T(8,128)} fusion(bf16[2048,2304]{1,0:T(8,128)(2,1)} %all-gather.3.cloned.1.call-done, bf16[1,2,2304,720]{2,3,1,0:T(8,128)(2,1)} %param.14), kind=kOutput, calls=%fused_computation.9 | convolution fusion | flops 6794772480 | bytes 18653184 | tf_op jit(solution)/shard_map/dot_general | solution.py:87
  142.8 28.4 %all-reduce.3.cloned.1.call-done = bf16[2048,32]{0,1:T(8,128)(2,1)} async-done(((bf16[2048,32]{0,1:T(8,128)(2,1)}), bf16[2048,32]{0,1:T(8,128)(2,1)}) %all-reduce.3.cloned.1.call-update) | async-done | bytes 131088 | tf_op jit(solution)/shard_map/psum | solution.py:77
  172.1 3.7 %broadcast_multiply_fusion = (bf16[2048,64,16]{0,2,1:T(8,128)(2,1)}, bf16[2048,64,16]{0,2,1:T(8,128)(2,1)S(1)}) fusion(bf16[2048,16]{0,1:T(8,128)(2,1)S(1)} %get-tuple-element.7, bf16[2048,64]{0,1:T(8,128)(2,1)} %fusion.27, bf16[2048,16]{0,1:T(8,128)(2,1)S(1)} %get-tuple-element.8), kind=kLoop, calls=%fused_computation.15 | loop fusion | flops 4194304 | bytes 8781824 | tf_op jit(solution)/shard_map/mul | solution.py:84
  175.8 5.2 %fusion.15 = f32[2048,720]{0,1:T(8,128)} fusion(bf16[2048,1024]{0,1:T(8,128)(2,1)S(1)} %bitcast.61, bf16[1,2,1024,720]{2,3,1,0:T(8,128)(2,1)S(1)} %copy-done.2), kind=kOutput, calls=%fused_computation.18 | convolution fusion | flops 3019898880 | bytes 11567104 | tf_op jit(solution)/shard_map/dot_general | solution.py:87
  181.0 18.9 %convolution_convert_fusion = bf16[2048,2304]{1,0:T(8,128)(2,1)} fusion(bf16[1,720,2304]{2,1,0:T(8,128)(2,1)S(1)} %copy-done, f32[2048,720]{0,1:T(8,128)} %fusion.3, f32[2048,720]{0,1:T(8,128)} %fusion.5, f32[2048,720]{0,1:T(8,128)} %fusion.15, bf16[2048,1024]{0,1:T(8,128)(2,1)} %bitcast.60, bf16[1,2,1024,720]{2,3,1,0:T(8,128)(2,1)} %param.17), kind=kOutput, calls=%fused_computation | convolution fusion | flops 9831186432 | bytes 36118528 | tf_op jit(solution)/shard_map/dot_general | solution.py:95
  199.9 76.0 %reduce-scatter.2.cloned.1.call-done = bf16[256,2304]{1,0:T(8,128)(2,1)} async-done(((bf16[2048,2304]{1,0:T(8,128)(2,1)}), bf16[256,2304]{1,0:T(8,128)(2,1)}) %reduce-scatter.2.cloned.1.call-update) | async-done | bytes 1179664 | tf_op jit(solution)/shard_map/reduce_scatter | solution.py:94
  276.0 4.6 %all-to-all-start.2 = ((bf16[4,64,2304]{2,1,0:T(8,128)(2,1)}), bf16[4,64,2304]{2,1,0:T(8,128)(2,1)}, u32[]{:S(2)}, u32[]{:S(2)}) async-start(bf16[4,64,2304]{2,1,0:T(8,128)(2,1)} %bitcast.63), calls=%async_computation.3 | async-start | bytes 2359296 | tf_op jit(solution)/shard_map/all_to_all | solution.py:103
  280.7 28.5 %all-to-all-done.2 = bf16[4,64,2304]{2,1,0:T(8,128)(2,1)} async-done(((bf16[4,64,2304]{2,1,0:T(8,128)(2,1)}), bf16[4,64,2304]{2,1,0:T(8,128)(2,1)}, u32[]{:S(2)}, u32[]{:S(2)}) %all-to-all-start.2) | async-done | bytes 1179680 | tf_op jit(solution)/shard_map/all_to_all | solution.py:103
  309.2 1.7 fusion.20
  311.0 1.9 fusion.26
  (49 shorter events, 5.3 us)
Async XLA Ops:
  6.5 174.4 %copy-start = (bf16[1,720,2304]{2,1,0:T(8,128)(2,1)S(1)}, bf16[1,720,2304]{2,1,0:T(8,128)(2,1)}, u32[]{:S(2)}) copy-start(bf16[1,720,2304]{2,1,0:T(8,128)(2,1)} %param.15) | copy-start | bytes 9953284
  6.5 104.2 %all-gather.3.cloned.1.call-start = ((), (), s32[]{:S(2)}) async-start(), calls=%async_computation.4 | async-start | bytes 10616832 | tf_op jit(solution)/shard_map/all_gather | solution.py:64
  11.7 41.0 %copy-start.3 = (s32[1,4]{1,0:T(1,128)S(1)}, s32[1,4]{1,0:T(1,128)}, u32[]{:S(2)}) copy-start(s32[1,4]{1,0:T(1,128)} %param.12) | copy-start | bytes 52
  11.7 41.2 %copy-start.4 = (s32[1,4]{1,0:T(1,128)S(1)}, s32[1,4]{1,0:T(1,128)}, u32[]{:S(2)}) copy-start(s32[1,4]{1,0:T(1,128)} %param.13) | copy-start | bytes 52
  54.1 8.7 %all-to-all-start.1 = ((bf16[4,1,64]{2,1,0:T(2,128)(2,1)}), bf16[4,1,64]{2,1,0:T(2,128)(2,1)S(1)}, u32[]{:S(2)}, u32[]{:S(2)}) async-start(bf16[4,1,64]{2,1,0:T(2,128)(2,1)} %all_to_all.16), calls=%async_computation.1 | async-start | bytes 4096 | tf_op jit(solution)/shard_map/all_to_all | solution.py:61
  57.4 113.8 %all-reduce.3.cloned.1.call-start = ((), (), s32[]{:S(2)}) async-start(), calls=%async_computation.5 | async-start | bytes 262144 | tf_op jit(solution)/shard_map/psum | solution.py:77
  118.1 157.9 %reduce-scatter.2.cloned.1.call-start = ((), (), s32[]{:S(2)}) async-start(), calls=%async_computation.6 | async-start | bytes 10616832 | tf_op jit(solution)/shard_map/reduce_scatter | solution.py:94
  172.1 3.7 %copy-start.2 = (bf16[1,2,1024,720]{2,3,1,0:T(8,128)(2,1)S(1)}, bf16[1,2,1024,720]{2,3,1,0:T(8,128)(2,1)}, u32[]{:S(2)}) copy-start(bf16[1,2,1024,720]{2,3,1,0:T(8,128)(2,1)} %param.17) | copy-start | bytes 8847364
  199.9 109.3 %copy-start.1 = (f32[96,2]{0,1:T(2,128)S(1)}, f32[96,2]{0,1:T(2,128)}, u32[]{:S(2)}) copy-start(f32[96,2]{0,1:T(2,128)} %param.11) | copy-start | bytes 2308
  276.0 33.2 %all-to-all-start.2 = ((bf16[4,64,2304]{2,1,0:T(8,128)(2,1)}), bf16[4,64,2304]{2,1,0:T(8,128)(2,1)}, u32[]{:S(2)}, u32[]{:S(2)}) async-start(bf16[4,64,2304]{2,1,0:T(8,128)(2,1)} %bitcast.63), calls=%async_computation.3 | async-start | bytes 2359296 | tf_op jit(solution)/shard_map/all_to_all | solution.py:103
Sparse Core Ops, SparseCore 0:
  52.8 57.9 all-gather.2
  118.2 52.9 all-reduce.2
  200.1 75.8 reduce-scatter.1
where the time goes:
time: 320 us; the launch traced here: 319 us
  waiting for transfers between devices  174 us (54%)
  matrix products  59.4 us (19%)
  blocking collectives  43.7 us (14%)
  between operations  13.3 us (4%)
  other arithmetic  10.7 us (3%)
  local copies, waits for them, and re-layouts  10.3 us (3%)
  starting transfers between devices  8.09 us (3%)
    reduce_scatter x1, waiting for transfers between devices, body(): lax.psum_scatter(jnp.dot(hidden_activations, expert_down[0], preferred_el...  76 us
    all_gather x1, waiting for transfers between devices, body(): lax.all_gather(arrived.reshape(-1, width), 'dp', axis=0, tiled=True)  38.1 us
    all_to_all x1, blocking collectives, body(): lax.all_to_all(outgoing, 'expert', split_axis=0, concat_axis=0, tiled=True)  34.8 us
    all_to_all x1, waiting for transfers between devices, body(): lax.all_to_all(mine, 'expert', split_axis=0, concat_axis=0, tiled=True)  28.5 us
    psum x1, waiting for transfers between devices, body(): lowrank = lax.psum(lowrank_part.astype(jnp.bfloat16), 'dp')  28.4 us
    dot_general x1, matrix products, body(): jnp.dot(hidden_activations, expert_down[0], preferred_element_type=jnp.fl...  18.9 us
    dot_general x1, matrix products, body(): jnp.dot(rows, expert_weights[0, 0], preferred_element_type=jnp.float32)  12.2 us
    dot_general x1, matrix products, body(): jnp.dot(rows, expert_weights[0, 1], preferred_element_type=jnp.float32)  12.2 us
  transfers between devices with their start and end apart: 5, of which 5 were waited for; matrix products, arithmetic and copies ran while one was open for 9% of the time, Pallas kernels for 0%

commit v1 on v0

--- a/solution.py
+++ b/solution.py
@@ -5,6 +5,24 @@
 
 TOP = 2
 RANK = 16
+
+
+def collect(shard, axis, dim):
+    ways, here, step = (lax.axis_size(axis), lax.axis_index(axis), shard.shape[dim])
+    dims = [n * ways if d == dim else n for d, n in enumerate(shard.shape)]
+    full = lax.dynamic_update_slice_in_dim(
+        jnp.zeros(dims, shard.dtype), shard, here * step, axis=dim
+    )
+    going_up = going_down = shard
+    for far in range(1, ways // 2 + 1):
+        going_up = lax.ppermute(going_up, axis, [(d, (d + 1) % ways) for d in range(ways)])
+        full = lax.dynamic_update_slice_in_dim(full, going_up, (here - far) % ways * step, axis=dim)
+        if 2 * far < ways:
+            going_down = lax.ppermute(going_down, axis, [(d, (d - 1) % ways) for d in range(ways)])
+            full = lax.dynamic_update_slice_in_dim(
+                full, going_down, (here + far) % ways * step, axis=dim
+            )
+    return full
 
 
 def body(
@@ -62,7 +80,7 @@
     )
     rows, labels_wire = (
         lax.all_gather(arrived.reshape(-1, width), "dp", axis=0, tiled=True),
-        lax.all_gather(arrived_ids.reshape(-1), "dp", axis=0, tiled=True),
+        collect(arrived_ids.reshape(-1), "dp", 0),
     )
     rows_total = rows.shape[0]
     labels = labels_wire.astype(jnp.int32)

time: 320 us -> 320 us (level)
  blocking collectives: 43.7 us -> 34.8 us
  starting transfers between devices: 8.09 us -> 16 us
    all_gather x1 -> x0, blocking collectives: 8.9 us -> none  [body(): lax.all_gather(arrived_ids.reshape(-1), 'dp', axis=0, tiled=True)]
    all_gather x1, waiting for transfers between devices: 38.1 us -> 30.1 us  [body(): lax.all_gather(arrived.reshape(-1, width), 'dp', axis=0, tiled=True)]
    ppermute x0 -> x7, starting transfers between devices: none -> 7.94 us  [the longest x3 7.93 us: collect(): lax.ppermute(going_down, axis, [(d, (d - 1) % ways) for d in range(ways)])]
    ppermute x0 -> x7, waiting for transfers between devices: none -> 4.93 us  [the longest x4 3.61 us: collect(): lax.ppermute(going_up, axis, [(d, (d + 1) % ways) for d in range(ways)])]
  transfers between devices with their start and end apart: 5 -> 12, of which waited for: 5 -> 8; matrix products, arithmetic and copies ran while one was open for 9% -> 9% of each run, Pallas kernels for 0% -> 0%
where the time goes in v1:
time: 320 us; the launch traced here: 319 us
  waiting for transfers between devices  173 us (54%)
  matrix products  59.4 us (19%)
  blocking collectives  34.8 us (11%)
  starting transfers between devices  16 us (5%)
  between operations  13.4 us (4%)
  local copies, waits for them, and re-layouts  11.8 us (4%)
  other arithmetic  10.7 us (3%)
    reduce_scatter x1, waiting for transfers between devices, body(): lax.psum_scatter(jnp.dot(hidden_activations, expert_down[0], preferred_el...  76 us
    all_to_all x1, blocking collectives, body(): lax.all_to_all(outgoing, 'expert', split_axis=0, concat_axis=0, tiled=True)  34.8 us
    all_gather x1, waiting for transfers between devices, body(): lax.all_gather(arrived.reshape(-1, width), 'dp', axis=0, tiled=True)  30.1 us
    all_to_all x1, waiting for transfers between devices, body(): lax.all_to_all(mine, 'expert', split_axis=0, concat_axis=0, tiled=True)  28.5 us
    psum x1, waiting for transfers between devices, body(): lowrank = lax.psum(lowrank_part.astype(jnp.bfloat16), 'dp')  28.4 us
    dot_general x1, matrix products, body(): jnp.dot(hidden_activations, expert_down[0], preferred_element_type=jnp.fl...  18.9 us
    dot_general x1, matrix products, body(): jnp.dot(rows, expert_weights[0, 0], preferred_element_type=jnp.float32)  12.2 us
    dot_general x1, matrix products, body(): jnp.dot(rows, expert_weights[0, 1], preferred_element_type=jnp.float32)  12.2 us
  transfers between devices with their start and end apart: 12, of which 8 were waited for; matrix products, arithmetic and copies ran while one was open for 9% of the time, Pallas kernels for 0%

profile of v1, /device:TPU:0, one launch (start us, length us, event | category | flops | bytes accessed | tf_op | source)
XLA Modules:
  0.0 319.3 jit_solution(6643834911162599803)
XLA Ops:
  11.7 1.4 broadcast_in_dim.6
  13.1 3.1 reshape.195
  16.2 1.6 convolution_convert_fusion.1
  17.9 34.8 %all_to_all.20 = bf16[4,64,2304]{2,1,0:T(8,128)(2,1)} all-to-all(bf16[4,64,2304]{2,1,0:T(8,128)(2,1)S(1)} %bitcast.57), channel_id=1, replica_groups=mesh['expert'=4,'dp'=8] {'expert'}, dimensions={0} | all-to-all | bytes 2359296 | tf_op jit(solution)/shard_map/all_to_all | solution.py:78
  54.1 3.2 %all-to-all-start.1 = ((bf16[4,1,64]{2,1,0:T(2,128)(2,1)}), bf16[4,1,64]{2,1,0:T(2,128)(2,1)S(1)}, u32[]{:S(2)}, u32[]{:S(2)}) async-start(bf16[4,1,64]{2,1,0:T(2,128)(2,1)} %all_to_all.16), calls=%async_computation.1 | async-start | bytes 4096 | tf_op jit(solution)/shard_map/all_to_all | solution.py:79
  57.5 5.3 %all-to-all-done.1 = bf16[4,1,64]{2,1,0:T(2,128)(2,1)S(1)} async-done(((bf16[4,1,64]{2,1,0:T(2,128)(2,1)}), bf16[4,1,64]{2,1,0:T(2,128)(2,1)S(1)}, u32[]{:S(2)}, u32[]{:S(2)}) %all-to-all-start.1) | async-done | bytes 544 | tf_op jit(solution)/shard_map/all_to_all | solution.py:79
  62.9 2.6 collective-permute-start.1
  66.8 2.4 copy.28
  69.2 2.6 collective-permute-start.3
  73.1 2.6 collective-permute-start.5
  77.2 2.4 collective-permute-done.6
  80.6 30.1 %all-gather.2.cloned.1.call-done = bf16[2048,2304]{1,0:T(8,128)(2,1)} async-done(((bf16[256,2304]{1,0:T(8,128)(2,1)}), bf16[2048,2304]{1,0:T(8,128)(2,1)}) %all-gather.2.cloned.1.call-update) | async-done | bytes 9437200 | tf_op jit(solution)/shard_map/all_gather | solution.py:82
  110.8 7.3 %fusion.21 = bf16[2048,32]{0,1:T(8,128)(2,1)} fusion(bf16[8,32,2304]{2,1,0:T(8,128)(2,1)} %bitcast.61, bf16[2048,2304]{1,0:T(8,128)(2,1)} %all-gather.2.cloned.1.call-done, f32[2048,8]{0,1:T(8,128)S(1)} %compare_convert_fusion), kind=kOutput, calls=%fused_computation.23 | convolution fusion | flops 2416902144 | bytes 10813440 | tf_op jit(solution)/shard_map/dot_general | solution.py:88
  118.3 12.2 %fusion.3 = f32[2048,720]{0,1:T(8,128)} fusion(bf16[2048,2304]{1,0:T(8,128)(2,1)} %all-gather.2.cloned.1.call-done, bf16[1,2,2304,720]{2,3,1,0:T(8,128)(2,1)} %param.14), kind=kOutput, calls=%fused_computation.7 | convolution fusion | flops 6794772480 | bytes 18653184 | tf_op jit(solution)/shard_map/dot_general | solution.py:108
  130.5 12.2 %fusion.5 = f32[2048,720]{0,1:T(8,128)} fusion(bf16[2048,2304]{1,0:T(8,128)(2,1)} %all-gather.2.cloned.1.call-done, bf16[1,2,2304,720]{2,3,1,0:T(8,128)(2,1)} %param.14), kind=kOutput, calls=%fused_computation.9 | convolution fusion | flops 6794772480 | bytes 18653184 | tf_op jit(solution)/shard_map/dot_general | solution.py:105
  142.7 28.4 %all-reduce.3.cloned.1.call-done = bf16[2048,32]{0,1:T(8,128)(2,1)} async-done(((bf16[2048,32]{0,1:T(8,128)(2,1)}), bf16[2048,32]{0,1:T(8,128)(2,1)}) %all-reduce.3.cloned.1.call-update) | async-done | bytes 131088 | tf_op jit(solution)/shard_map/psum | solution.py:95
  172.1 3.7 %broadcast_multiply_fusion = (bf16[2048,64,16]{0,2,1:T(8,128)(2,1)}, bf16[2048,64,16]{0,2,1:T(8,128)(2,1)S(1)}) fusion(bf16[2048,16]{0,1:T(8,128)(2,1)S(1)} %get-tuple-element.7, bf16[2048,64]{0,1:T(8,128)(2,1)} %fusion.27, bf16[2048,16]{0,1:T(8,128)(2,1)S(1)} %get-tuple-element.8), kind=kLoop, calls=%fused_computation.15 | loop fusion | flops 4194304 | bytes 8781824 | tf_op jit(solution)/shard_map/mul | solution.py:102
  175.8 5.2 %fusion.15 = f32[2048,720]{0,1:T(8,128)} fusion(bf16[2048,1024]{0,1:T(8,128)(2,1)S(1)} %bitcast.60, bf16[1,2,1024,720]{2,3,1,0:T(8,128)(2,1)S(1)} %copy-done.2), kind=kOutput, calls=%fused_computation.18 | convolution fusion | flops 3019898880 | bytes 11567104 | tf_op jit(solution)/shard_map/dot_general | solution.py:105
  181.0 18.9 %convolution_convert_fusion = bf16[2048,2304]{1,0:T(8,128)(2,1)} fusion(bf16[1,720,2304]{2,1,0:T(8,128)(2,1)S(1)} %copy-done, f32[2048,720]{0,1:T(8,128)} %fusion.3, f32[2048,720]{0,1:T(8,128)} %fusion.5, f32[2048,720]{0,1:T(8,128)} %fusion.15, bf16[2048,1024]{0,1:T(8,128)(2,1)} %bitcast.59, bf16[1,2,1024,720]{2,3,1,0:T(8,128)(2,1)} %param.17), kind=kOutput, calls=%fused_computation | convolution fusion | flops 9831186432 | bytes 36118528 | tf_op jit(solution)/shard_map/dot_general | solution.py:113
  199.9 76.0 %reduce-scatter.2.cloned.1.call-done = bf16[256,2304]{1,0:T(8,128)(2,1)} async-done(((bf16[2048,2304]{1,0:T(8,128)(2,1)}), bf16[256,2304]{1,0:T(8,128)(2,1)}) %reduce-scatter.2.cloned.1.call-update) | async-done | bytes 1179664 | tf_op jit(solution)/shard_map/reduce_scatter | solution.py:112
  275.9 4.6 %all-to-all-start.2 = ((bf16[4,64,2304]{2,1,0:T(8,128)(2,1)}), bf16[4,64,2304]{2,1,0:T(8,128)(2,1)}, u32[]{:S(2)}, u32[]{:S(2)}) async-start(bf16[4,64,2304]{2,1,0:T(8,128)(2,1)} %bitcast.62), calls=%async_computation.3 | async-start | bytes 2359296 | tf_op jit(solution)/shard_map/all_to_all | solution.py:121
  280.7 28.5 %all-to-all-done.2 = bf16[4,64,2304]{2,1,0:T(8,128)(2,1)} async-done(((bf16[4,64,2304]{2,1,0:T(8,128)(2,1)}), bf16[4,64,2304]{2,1,0:T(8,128)(2,1)}, u32[]{:S(2)}, u32[]{:S(2)}) %all-to-all-start.2) | async-done | bytes 1179680 | tf_op jit(solution)/shard_map/all_to_all | solution.py:121
  309.2 1.7 fusion.20
  310.9 1.9 fusion.26
  (71 shorter events, 13.1 us)
Async XLA Ops:
  6.5 174.4 %copy-start = (bf16[1,720,2304]{2,1,0:T(8,128)(2,1)S(1)}, bf16[1,720,2304]{2,1,0:T(8,128)(2,1)}, u32[]{:S(2)}) copy-start(bf16[1,720,2304]{2,1,0:T(8,128)(2,1)} %param.15) | copy-start | bytes 9953284
  6.5 104.2 %all-gather.2.cloned.1.call-start = ((), (), s32[]{:S(2)}) async-start(), calls=%async_computation.4 | async-start | bytes 10616832 | tf_op jit(solution)/shard_map/all_gather | solution.py:82
  11.7 41.0 %copy-start.3 = (s32[1,4]{1,0:T(1,128)S(1)}, s32[1,4]{1,0:T(1,128)}, u32[]{:S(2)}) copy-start(s32[1,4]{1,0:T(1,128)} %param.12) | copy-start | bytes 52
  11.7 41.2 %copy-start.4 = (s32[1,4]{1,0:T(1,128)S(1)}, s32[1,4]{1,0:T(1,128)}, u32[]{:S(2)}) copy-start(s32[1,4]{1,0:T(1,128)} %param.13) | copy-start | bytes 52
  54.1 8.7 %all-to-all-start.1 = ((bf16[4,1,64]{2,1,0:T(2,128)(2,1)}), bf16[4,1,64]{2,1,0:T(2,128)(2,1)S(1)}, u32[]{:S(2)}, u32[]{:S(2)}) async-start(bf16[4,1,64]{2,1,0:T(2,128)(2,1)} %all_to_all.16), calls=%async_computation.1 | async-start | bytes 4096 | tf_op jit(solution)/shard_map/all_to_all | solution.py:79
  57.4 113.8 %all-reduce.3.cloned.1.call-start = ((), (), s32[]{:S(2)}) async-start(), calls=%async_computation.5 | async-start | bytes 262144 | tf_op jit(solution)/shard_map/psum | solution.py:95
  62.9 3.9 %collective-permute-start = (bf16[256]{0:T(256)(128)(2,1)S(1)}, bf16[256]{0:T(256)(128)(2,1)S(1)}, u32[]{:S(2)}, u32[]{:S(2)}) collective-permute-start(bf16[256]{0:T(256)(128)(2,1)S(1)} %reshape.200), channel_id=1, source_target_pairs={{0,1},{1,2},{2,3},{3,4},{4,5},{5,6},{6,7},{7,0},{8,9},{9,10},{10,1... | collective-permute-start | bytes 1544 | tf_op jit(solution)/shard_map/ppermute | solution.py:18
  62.9 6.2 %collective-permute-start.1 = (bf16[256]{0:T(256)(128)(2,1)S(1)}, bf16[256]{0:T(256)(128)(2,1)S(1)}, u32[]{:S(2)}, u32[]{:S(2)}) collective-permute-start(bf16[256]{0:T(256)(128)(2,1)S(1)} %reshape.200), channel_id=1, source_target_pairs={{0,7},{1,0},{2,1},{3,2},{4,3},{5,4},{6,5},{7,6},{8,15},{9,8},{10,9... | collective-permute-start | bytes 1544 | tf_op jit(solution)/shard_map/ppermute | solution.py:21
  66.8 5.0 %collective-permute-start.2 = (bf16[256]{0:T(256)(128)(2,1)S(1)}, bf16[256]{0:T(256)(128)(2,1)S(1)}, u32[]{:S(2)}, u32[]{:S(2)}) collective-permute-start(bf16[256]{0:T(256)(128)(2,1)S(1)} %collective-permute-done), channel_id=1, source_target_pairs={{0,1},{1,2},{2,3},{3,4},{4,5},{5,6},{6,7},{7,0},{8,9},{9,10},{10,1... | collective-permute-start | bytes 1544 | tf_op jit(solution)/shard_map/ppermute | solution.py:18
  69.2 3.9 %collective-permute-start.3 = (bf16[256]{0:T(256)(128)(2,1)S(1)}, bf16[256]{0:T(256)(128)(2,1)S(1)}, u32[]{:S(2)}, u32[]{:S(2)}) collective-permute-start(bf16[256]{0:T(256)(128)(2,1)S(1)} %collective-permute-done.1), channel_id=1, source_target_pairs={{0,7},{1,0},{2,1},{3,2},{4,3},{5,4},{6,5},{7,6},{8,15},{9,8},{10,9... | collective-permute-start | bytes 1544 | tf_op jit(solution)/shard_map/ppermute | solution.py:21
  71.8 3.9 %collective-permute-start.4 = (bf16[256]{0:T(256)(128)(2,1)S(1)}, bf16[256]{0:T(256)(128)(2,1)S(1)}, u32[]{:S(2)}, u32[]{:S(2)}) collective-permute-start(bf16[256]{0:T(256)(128)(2,1)S(1)} %collective-permute-done.2), channel_id=1, source_target_pairs={{0,1},{1,2},{2,3},{3,4},{4,5},{5,6},{6,7},{7,0},{8,9},{9,10},{10,1... | collective-permute-start | bytes 1544 | tf_op jit(solution)/shard_map/ppermute | solution.py:18
  73.1 3.9 %collective-permute-start.5 = (bf16[256]{0:T(256)(128)(2,1)S(1)}, bf16[256]{0:T(256)(128)(2,1)S(1)}, u32[]{:S(2)}, u32[]{:S(2)}) collective-permute-start(bf16[256]{0:T(256)(128)(2,1)S(1)} %collective-permute-done.3), channel_id=1, source_target_pairs={{0,7},{1,0},{2,1},{3,2},{4,3},{5,4},{6,5},{7,6},{8,15},{9,8},{10,9... | collective-permute-start | bytes 1544 | tf_op jit(solution)/shard_map/ppermute | solution.py:21
  75.7 3.9 %collective-permute-start.6 = (bf16[256]{0:T(256)(128)(2,1)S(1)}, bf16[256]{0:T(256)(128)(2,1)S(1)}, u32[]{:S(2)}, u32[]{:S(2)}) collective-permute-start(bf16[256]{0:T(256)(128)(2,1)S(1)} %collective-permute-done.4), channel_id=1, source_target_pairs={{0,1},{1,2},{2,3},{3,4},{4,5},{5,6},{6,7},{7,0},{8,9},{9,10},{10,1... | collective-permute-start | bytes 1544 | tf_op jit(solution)/shard_map/ppermute | solution.py:18
  118.1 157.9 %reduce-scatter.2.cloned.1.call-start = ((), (), s32[]{:S(2)}) async-start(), calls=%async_computation.6 | async-start | bytes 10616832 | tf_op jit(solution)/shard_map/reduce_scatter | solution.py:112
  172.1 3.7 %copy-start.2 = (bf16[1,2,1024,720]{2,3,1,0:T(8,128)(2,1)S(1)}, bf16[1,2,1024,720]{2,3,1,0:T(8,128)(2,1)}, u32[]{:S(2)}) copy-start(bf16[1,2,1024,720]{2,3,1,0:T(8,128)(2,1)} %param.17) | copy-start | bytes 8847364
  199.9 109.3 %copy-start.1 = (f32[96,2]{0,1:T(2,128)S(1)}, f32[96,2]{0,1:T(2,128)}, u32[]{:S(2)}) copy-start(f32[96,2]{0,1:T(2,128)} %param.11) | copy-start | bytes 2308
  275.9 33.2 %all-to-all-start.2 = ((bf16[4,64,2304]{2,1,0:T(8,128)(2,1)}), bf16[4,64,2304]{2,1,0:T(8,128)(2,1)}, u32[]{:S(2)}, u32[]{:S(2)}) async-start(bf16[4,64,2304]{2,1,0:T(8,128)(2,1)} %bitcast.62), calls=%async_computation.3 | async-start | bytes 2359296 | tf_op jit(solution)/shard_map/all_to_all | solution.py:121
Sparse Core Ops, SparseCore 0:
  52.8 57.9 all-gather.1
  118.2 52.9 all-reduce.2
  200.1 75.8 reduce-scatter.1
